TPU v7x, 1024 devices: a whole 8x8x8 slice. The times are simulated.
1024 devices in a mesh: leaf: 64 (over x, z), sub: 16 (over y, core).
Axes of the slice: x: 8, y: 8, z: 8, core: 2. Of those that a mesh axis runs over, the one named last changes fastest.
Arguments:
- coarse_scaling: float32 [512, 131072], P(None, ('leaf', 'sub')), may hold values from -6 to 6
- details: bfloat16 [2, 3584, 131072], P(None, None, ('leaf', 'sub')), may hold values from -6 to 6
- two_scale: float32 [16, 16], replicated, may hold values from -1 to 1, as said below
- parent_link: int32 [2, 131072], P(None, ('leaf', 'sub')), may hold values from -1 to 1048575, as said below
Outputs:
- leaf_scaling: float32 [512, 131072], P(None, ('leaf', 'sub'))
Inputs may be any that keep to these rules, and one draw needn't show every extreme that they name: `parent_link`: slots are numbered leaf-major over the devices, 128 to a device. A box that has children has all eight, in eight consecutive slots in octant order. A box's parent stands on the same device, or in the last 4 slots of the previous device; each of those 4 boxes (except on the last device) has its eight children in the last 32 slots of the next device, and none on its own. Parents are live boxes (the level above has a link that is not -1, or is level 0). The last 4 slots of every device are live at every level. `two_scale`: an orthogonal matrix.
All inputs are finite; a program needn't handle non-finite values.
Results may differ from a plain program's by a relative error of at most 0.0003.
Values sent between devices are 32-bit elements; how exact they have to be, the bound alone decides.
A program may use at most 128 MiB of HBM per device.

v0:
```python
import jax
import jax.numpy as jnp
from jax import lax
from jax.sharding import PartitionSpec as P

TAIL = 4
LEVELS = 2


def from_behind(x, axis, by):
    size = lax.axis_size(axis)
    pairs = [(i, i + by) for i in range(size) if 0 <= i + by < size]
    return lax.ppermute(x, axis, pairs)


def unfilter(two_scale, scaling, wavelet):
    box_count = scaling.shape[1]
    poly_order = two_scale.shape[0] // 2
    coefficients = jnp.concatenate([scaling, wavelet], 0).reshape(
        2, 2, 2, poly_order, poly_order, poly_order, box_count
    )
    halves = two_scale.reshape(2, poly_order, 2, poly_order)
    precise = lax.Precision.HIGHEST
    first_pass = jnp.einsum("PIai,abcijkn->PIbcjkn", halves, coefficients, precision=precise)
    second_pass = jnp.einsum("QJbj,PIbcjkn->PIQJckn", halves, first_pass, precision=precise)
    third_pass = jnp.einsum("RMck,PIQJckn->IJMnPQR", halves, second_pass, precision=precise)
    return third_pass.reshape(poly_order * poly_order * poly_order, box_count * 8)


def on_device(coarse_scaling, details, two_scale, parent_link):
    slot_count = coarse_scaling.shape[1]
    boundary = slot_count - TAIL
    device = lax.axis_index(("leaf", "sub"))
    first_child = device * (slot_count * 8)
    spread = (slot_count + TAIL) * 8
    scaling = coarse_scaling
    for level_index in range(LEVELS):
        wavelet = details[level_index].astype(jnp.float32)
        own_children = unfilter(two_scale, scaling, wavelet)
        received = from_behind(own_children[:, 8 * boundary :], ("leaf", "sub"), 1)
        candidates = jnp.concatenate([own_children, received], 1)
        parent_rows = parent_link[level_index]
        offset = parent_rows - first_child
        position = jnp.clip(jnp.where(offset >= 0, offset, offset + spread), 0, spread - 1)
        picked = jnp.take(candidates, position, axis=1)
        scaling = jnp.where(parent_rows[None, :] >= 0, picked, 0.0)
    return scaling


def solution(mesh):
    placed = (
        P(None, ("leaf", "sub")),
        P(None, None, ("leaf", "sub")),
        P(),
        P(None, ("leaf", "sub")),
    )
    return jax.shard_map(
        on_device, mesh=mesh, in_specs=placed, out_specs=P(None, ("leaf", "sub")), check_vma=False
    )
```

profile of v0, /device:TPU:14, one launch (start us, length us, event | category | flops | bytes accessed | tf_op | source)
XLA Modules:
  0.0 162.8 jit_solution(1287043877674659874)
XLA Ops:
  0.0 0.0 copy-start.2
  0.0 0.0 copy-start.1
  0.0 3.0 %bitcast_convert_fusion.1 = (f32[3584,128]{1,0:T(8,128)S(1)}, f32[3584,128]{1,0:T(8,128)}) fusion(bf16[2,3584,128]{2,1,0:T(8,128)(2,1)} %param.7), kind=kLoop, calls=%fused_computation.25 | loop fusion | flops 917504 | bytes 5505024 | tf_op jit(solution)/shard_map/convert_element_type | solution.py:38
  3.0 0.0 copy-done.2
  3.0 0.1 reshape.30
  3.0 0.0 copy-done.1
  3.0 0.1 pad_maximum_fusion.2
  3.2 3.1 %fusion.12 = f32[2,8,2,2,8,8,128,1]{6,1,0,5,4,3,2,7:T(8,128)S(1)} fusion(f32[2,2,2,8,8,8,128,1]{6,5,4,3,2,1,0,7:T(8,128)S(1)} %bitcast.79, f32[2,8,2,8,1,1,1,1]{3,2,1,0,7,6,5,4:T(2,128)S(1)} %bitcast.80), kind=kOutput, calls=%fused_computation.18 | convolution fusion | flops 100663296 | bytes 4195328 | tf_op jit(solution)/shard_map/PIai,abcijkn->PIbcjkn/dot_general | solution.py:24
  6.3 3.3 %fusion.15 = f32[2,8,2,8,2,8,128,1]{6,3,2,5,4,1,0,7:T(8,128)S(1)} fusion(f32[2,8,2,2,8,8,128,1]{6,1,0,5,4,3,2,7:T(8,128)S(1)} %fusion.12, f32[2,8,2,8,1,1,1,1]{3,2,1,0,7,6,5,4:T(2,128)S(1)} %bitcast.81), kind=kOutput, calls=%fused_computation.19 | convolution fusion | flops 100663296 | bytes 4195328 | tf_op jit(solution)/shard_map/QJbj,PIbcjkn->PIQJckn/dot_general | solution.py:25
  9.6 2.4 %fusion.18 = f32[8,8,8,128,2,2,2]{3,2,6,1,5,0,4:T(8,128)S(1)} fusion(f32[2,8,2,8,2,8,128,1]{6,3,2,5,4,1,0,7:T(8,128)S(1)} %fusion.15, f32[2,8,2,8,1,1,1,1]{3,2,1,0,7,6,5,4:T(2,128)S(1)} %bitcast.82), kind=kOutput, calls=%fused_computation.20 | convolution fusion | flops 100663296 | bytes 4195328 | tf_op jit(solution)/shard_map/RMck,PIQJckn->IJMnPQR/dot_general | solution.py:26
  12.0 25.6 %copy.35 = f32[8,8,8,128,2,2,2]{2,1,0,6,5,4,3:T(8,128)} copy(f32[8,8,8,128,2,2,2]{3,2,6,1,5,0,4:T(8,128)S(1)} %fusion.18) | data formatting | bytes 4194304 | tf_op jit(solution)/shard_map/RMck,PIQJckn->IJMnPQR/transpose | solution.py:26
  37.7 24.0 %reshape.31 = f32[512,1024]{0,1:T(8,128)S(1)} reshape(f32[8,8,8,128,2,2,2]{2,1,0,6,5,4,3:T(8,128)} %copy.35) | data formatting | bytes 4194304 | tf_op jit(solution)/shard_map/reshape | solution.py:27
  61.7 1.9 %collective-permute-start = (f32[512,32]{0,1:T(8,128)S(1)}, f32[512,32]{0,1:T(8,128)S(1)}, u32[]{:S(2)}, u32[]{:S(2)}) collective-permute-start(f32[512,32]{0,1:T(8,128)S(1)} %slice.28), channel_id=1, source_target_pairs={{0,1},{1,2},{2,3},{3,4},{4,5},{5,6},{6,7},{7,8},{8,9},{9,10},{10,1... | collective-permute-start | bytes 196616 | tf_op jit(solution)/shard_map/ppermute | solution.py:13
  63.6 0.0 copy-done.3
  63.7 21.3 %collective-permute-done = f32[512,32]{0,1:T(8,128)S(1)} collective-permute-done((f32[512,32]{0,1:T(8,128)S(1)}, f32[512,32]{0,1:T(8,128)S(1)}, u32[]{:S(2)}, u32[]{:S(2)}) %collective-permute-start) | collective-permute-done | bytes 65568 | tf_op jit(solution)/shard_map/ppermute | solution.py:13
  84.9 1.5 pad_maximum_fusion
  86.5 2.6 %gather_fusion = f32[128,512]{1,0:T(8,128)S(1)} fusion(f32[512,1056]{0,1:T(8,128)} %pad_maximum_fusion, s32[1024]{0:T(1024)S(1)} %pad_clamp_fusion.1), kind=kCustom, calls=%fused_computation.clone | custom fusion | bytes 524800 | tf_op jit(solution)/shard_map/jit(_take)/gather | solution.py:45
  89.1 0.1 bitcast_select_fusion.1
  89.2 0.1 copy.36
  89.3 0.0 copy-done
  89.3 0.1 pad_maximum_fusion.3
  89.5 3.1 %fusion.21 = f32[2,8,2,2,8,8,128,1]{6,1,0,5,4,3,2,7:T(8,128)S(1)} fusion(f32[2,2,2,8,8,8,128,1]{6,5,4,3,2,1,0,7:T(8,128)S(1)} %bitcast.78, f32[2,8,2,8,1,1,1,1]{3,2,1,0,7,6,5,4:T(2,128)S(1)} %bitcast.83), kind=kOutput, calls=%fused_computation.21 | convolution fusion | flops 100663296 | bytes 4195328 | tf_op jit(solution)/shard_map/PIai,abcijkn->PIbcjkn/dot_general | solution.py:24
  92.6 3.3 %fusion.24 = f32[2,8,2,8,2,8,128,1]{6,3,2,5,4,1,0,7:T(8,128)S(1)} fusion(f32[2,8,2,2,8,8,128,1]{6,1,0,5,4,3,2,7:T(8,128)S(1)} %fusion.21, f32[2,8,2,8,1,1,1,1]{3,2,1,0,7,6,5,4:T(2,128)S(1)} %bitcast.84), kind=kOutput, calls=%fused_computation.22 | convolution fusion | flops 100663296 | bytes 4195328 | tf_op jit(solution)/shard_map/QJbj,PIbcjkn->PIQJckn/dot_general | solution.py:25
  95.9 2.4 %fusion.27 = f32[8,8,8,128,2,2,2]{3,2,6,1,5,0,4:T(8,128)S(1)} fusion(f32[2,8,2,8,2,8,128,1]{6,3,2,5,4,1,0,7:T(8,128)S(1)} %fusion.24, f32[2,8,2,8,1,1,1,1]{3,2,1,0,7,6,5,4:T(2,128)S(1)} %bitcast.85), kind=kOutput, calls=%fused_computation.23 | convolution fusion | flops 100663296 | bytes 4195328 | tf_op jit(solution)/shard_map/RMck,PIQJckn->IJMnPQR/dot_general | solution.py:26
  98.3 25.7 %copy.43 = f32[8,8,8,128,2,2,2]{2,1,0,6,5,4,3:T(8,128)} copy(f32[8,8,8,128,2,2,2]{3,2,6,1,5,0,4:T(8,128)S(1)} %fusion.27) | data formatting | bytes 4194304 | tf_op jit(solution)/shard_map/RMck,PIQJckn->IJMnPQR/transpose | solution.py:26
  124.0 24.0 %reshape.33 = f32[512,1024]{0,1:T(8,128)S(1)} reshape(f32[8,8,8,128,2,2,2]{2,1,0,6,5,4,3:T(8,128)} %copy.43) | data formatting | bytes 4194304 | tf_op jit(solution)/shard_map/reshape | solution.py:27
  148.0 1.9 %collective-permute-start.1 = (f32[512,32]{0,1:T(8,128)S(1)}, f32[512,32]{0,1:T(8,128)S(1)}, u32[]{:S(2)}, u32[]{:S(2)}) collective-permute-start(f32[512,32]{0,1:T(8,128)S(1)} %slice.29), channel_id=1, source_target_pairs={{0,1},{1,2},{2,3},{3,4},{4,5},{5,6},{6,7},{7,8},{8,9},{9,10},{10,1... | collective-permute-start | bytes 196616 | tf_op jit(solution)/shard_map/ppermute | solution.py:13
  149.9 7.9 %collective-permute-done.1 = f32[512,32]{0,1:T(8,128)S(1)} collective-permute-done((f32[512,32]{0,1:T(8,128)S(1)}, f32[512,32]{0,1:T(8,128)S(1)}, u32[]{:S(2)}, u32[]{:S(2)}) %collective-permute-start.1) | collective-permute-done | bytes 65568 | tf_op jit(solution)/shard_map/ppermute | solution.py:13
  157.8 1.5 pad_maximum_fusion.1
  159.3 2.5 %gather_fusion.1 = f32[128,512]{1,0:T(8,128)S(1)} fusion(f32[512,1056]{0,1:T(8,128)} %pad_maximum_fusion.1, s32[1024]{0:T(1024)S(1)} %pad_clamp_fusion), kind=kCustom, calls=%fused_computation.1.clone | custom fusion | bytes 524800 | tf_op jit(solution)/shard_map/jit(_take)/gather | solution.py:45
  161.8 0.1 bitcast_select_fusion
  161.9 0.8 copy.44
  (8 shorter events, 0.1 us)
Async XLA Ops:
  0.0 3.0 %copy-start.2 = (f32[16,16]{1,0:T(8,128)S(1)}, f32[16,16]{1,0:T(8,128)}, u32[]{:S(2)}) copy-start(f32[16,16]{1,0:T(8,128)} %param.8) | copy-start | bytes 3076
  0.0 3.0 %copy-start.1 = (f32[512,128]{1,0:T(8,128)S(1)}, f32[512,128]{1,0:T(8,128)}, u32[]{:S(2)}) copy-start(f32[512,128]{1,0:T(8,128)} %param.6) | copy-start | bytes 786436
  37.7 25.9 %copy-start.3 = (s32[2,128]{1,0:T(2,128)S(1)}, s32[2,128]{1,0:T(2,128)}, u32[]{:S(2)}) copy-start(s32[2,128]{1,0:T(2,128)} %param.9) | copy-start | bytes 3076
  61.7 23.3 %collective-permute-start = (f32[512,32]{0,1:T(8,128)S(1)}, f32[512,32]{0,1:T(8,128)S(1)}, u32[]{:S(2)}, u32[]{:S(2)}) collective-permute-start(f32[512,32]{0,1:T(8,128)S(1)} %slice.28), channel_id=1, source_target_pairs={{0,1},{1,2},{2,3},{3,4},{4,5},{5,6},{6,7},{7,8},{8,9},{9,10},{10,1... | collective-permute-start | bytes 196616 | tf_op jit(solution)/shard_map/ppermute | solution.py:13
  86.5 2.9 %copy-start = (f32[3584,128]{1,0:T(8,128)S(1)}, f32[3584,128]{1,0:T(8,128)}, u32[]{:S(2)}) copy-start(f32[3584,128]{1,0:T(8,128)} %get-tuple-element.11) | copy-start | bytes 5505028
  148.0 9.8 %collective-permute-start.1 = (f32[512,32]{0,1:T(8,128)S(1)}, f32[512,32]{0,1:T(8,128)S(1)}, u32[]{:S(2)}, u32[]{:S(2)}) collective-permute-start(f32[512,32]{0,1:T(8,128)S(1)} %slice.29), channel_id=1, source_target_pairs={{0,1},{1,2},{2,3},{3,4},{4,5},{5,6},{6,7},{7,8},{8,9},{9,10},{10,1... | collective-permute-start | bytes 196616 | tf_op jit(solution)/shard_map/ppermute | solution.py:13
where the time goes:
time: 164 us; the launch traced here: 163 us
  local copies, waits for them, and re-layouts  105 us (64%)
  waiting for transfers between devices  29.1 us (18%)
  matrix products  17.6 us (11%)
  other arithmetic  6.54 us (4%)
  starting transfers between devices  3.84 us (2%)
    transpose x2, local copies, waits for them, and re-layouts, unfilter(): jnp.einsum('RMck,PIQJckn->IJMnPQR', halves, second_pass, precision=precise)  51.3 us
    reshape x2, local copies, waits for them, and re-layouts, unfilter(): third_pass.reshape(poly_order * poly_order * poly_order, box_count * 8)  48 us
    ppermute x2, waiting for transfers between devices, from_behind(): return lax.ppermute(x, axis, pairs)  29.1 us
    dot_general x2, matrix products, unfilter(): jnp.einsum('QJbj,PIbcjkn->PIQJckn', halves, first_pass, precision=precise)  6.56 us
    dot_general x2, matrix products, unfilter(): jnp.einsum('PIai,abcijkn->PIbcjkn', halves, coefficients, precision=precise)  6.25 us
    gather x2, local copies, waits for them, and re-layouts, on_device(): picked = jnp.take(candidates, position, axis=1)  5.09 us
    dot_general x2, matrix products, unfilter(): jnp.einsum('RMck,PIQJckn->IJMnPQR', halves, second_pass, precision=precise)  4.83 us
    ppermute x2, starting transfers between devices, from_behind(): return lax.ppermute(x, axis, pairs)  3.84 us
  transfers between devices with their start and end apart: 2, of which 2 were waited for; matrix products, arithmetic and copies ran while one was open for 0% of the time, Pallas kernels for 0%

commit v1 on v0

v1 whole, which is shorter than its diff:
```python
import jax
import jax.numpy as jnp
from jax import lax
from jax.experimental import pallas as pl
from jax.experimental.pallas import tpu as pltpu
from jax.sharding import PartitionSpec as P

MESH = pl.DeviceIdType.MESH
TAIL = 4
F32, BF16, I32 = jnp.float32, jnp.bfloat16, jnp.int32


def iota(shape, axis):
    return lax.broadcasted_iota(I32, shape, axis)


def nn(a, b):
    return lax.dot_general(a, b, (((1,), (0,)), ((), ())), preferred_element_type=F32)


def nt(a, b):
    return lax.dot_general(a, b, (((1,), (1,)), ((), ())), preferred_element_type=F32)


def split(x):
    hi = x.astype(BF16)
    return hi, (x - hi.astype(F32)).astype(BF16)


def triple(dot, a, b):
    return dot(a[0], b[0]) + dot(a[1], b[0]) + dot(a[0], b[1])


def flag(mask):
    return jnp.where(mask, 1.0, 0.0)


def one_hot(mask):
    return flag(mask).astype(BF16)


def pick_exact(dot, parts, other):
    return dot(parts[0], other) + dot(parts[1], other) + dot(parts[2], other)


def thirds(x):
    hi, rest = x.astype(BF16), None
    rest = x - hi.astype(F32)
    mid = rest.astype(BF16)
    return hi, mid, (rest - mid.astype(F32)).astype(BF16)


def kernel(
    leafs, subs,
    coarse_hbm, details_hbm, w_ref, link_ref, out_ref,
    coarse, details, x_hi, x_lo, x2, as_hi, as_lo, send0, recv0, send1, recv1, send2, recv2,
    local_sem, send_sem, recv_sem,
):
    leaf, sub = lax.axis_index("leaf"), lax.axis_index("sub")
    device = leaf * subs + sub
    total = leafs * subs
    ahead = lax.rem(device + 1, total)
    behind = lax.rem(device + total - 1, total)
    target = (lax.div(ahead, subs), lax.rem(ahead, subs))
    source = (lax.div(behind, subs), lax.rem(behind, subs))

    load_coarse = pltpu.make_async_copy(coarse_hbm, coarse, local_sem.at[0])
    load_first = pltpu.make_async_copy(details_hbm.at[0], details.at[0], local_sem.at[1])
    load_second = pltpu.make_async_copy(details_hbm.at[1], details.at[1], local_sem.at[2])
    load_coarse.start()
    load_first.start()
    load_second.start()

    barrier = pltpu.get_barrier_semaphore()
    pl.semaphore_signal(barrier, inc=1, device_id=source, device_id_type=MESH)

    first_child = device * 1024
    slot = iota((1, 128), 1)

    def read_links(level):
        link = link_ref[level : level + 1, :]
        live = link >= 0
        own = link >= first_child
        offset = link - first_child
        parent = jnp.where(own, offset, offset + 8 * TAIL) >> 3
        octant = link & 7
        group = (slot - octant) >> 3
        return live, own, live & (link < first_child), parent, octant, group

    def parents_of(links):
        live, own, before, parent, octant, group = links
        start = own & (octant == 0)
        lead = one_hot(((slot >> 3) == iota((16, 128), 0)) & start)
        match = one_hot(iota((128, 128), 0) == parent)
        return nt(lead, match)

    links1, links2 = read_links(0), read_links(1)
    row32 = iota((16, 128), 0)
    tail_rows = (iota((16, 128), 1) == 128 - TAIL + (row32 & 3))
    chosen1, chosen2 = parents_of(links1), parents_of(links2)
    twice = flag(tail_rows & (row32 < 8))
    once = flag(tail_rows & (row32 < 4))
    pick1 = jnp.concatenate([chosen1, twice], 0).astype(BF16)
    pick2 = jnp.concatenate([chosen2, twice], 0).astype(BF16)
    slots2 = jnp.concatenate([chosen2, once], 0).astype(BF16)

    upper = iota((8, 256), 0) < 4

    def stacked(level, a, i):
        first = 64 * i
        return [details[level, pl.ds(512 * (4 * a + q - 1) + first, 64), :] for q in range(4) if 4 * a + q]

    load_coarse.wait()
    load_first.wait()
    no_rows = jnp.zeros((192, 128), BF16)
    pick1_twice = jnp.concatenate([pick1, pick1], 1)
    for i in range(8):
        hi, lo = split(coarse[pl.ds(64 * i, 64), :])
        blocks = jnp.concatenate([hi] + stacked(0, 0, i), 0)
        lower = jnp.concatenate([lo, no_rows], 0)
        even = nt(pick1_twice, jnp.concatenate([blocks, lower], 1))
        odd = nt(pick1, jnp.concatenate(stacked(0, 1, i), 0))
        e_hi, e_lo = split(even[:16])
        x_hi[pl.ds(16 * i, 16), :] = e_hi
        x_lo[pl.ds(16 * i, 16), :] = e_lo
        x_hi[pl.ds(128 + 16 * i, 16), :] = odd[:16].astype(BF16)
        send0[pl.ds(8 * i, 8), :] = jnp.where(upper, even[16:24], odd[16:24])

    def hop(n, src, dst):
        return pltpu.make_async_remote_copy(
            src_ref=src, dst_ref=dst, send_sem=send_sem.at[n], recv_sem=recv_sem.at[n],
            device_id=target, device_id_type=MESH,
        )

    hop0, hop1, hop2 = hop(0, send0, recv0), hop(1, send1, recv1), hop(2, send2, recv2)
    pl.semaphore_wait(barrier, 1)
    hop0.start()

    load_second.wait()
    for i in range(8):
        even = nt(pick2, jnp.concatenate([jnp.zeros((64, 128), BF16)] + stacked(1, 0, i), 0))
        odd = nt(pick2, jnp.concatenate(stacked(1, 1, i), 0))
        x2[pl.ds(16 * i, 16), :] = even[:16].astype(BF16)
        x2[pl.ds(128 + 16 * i, 16), :] = odd[:16].astype(BF16)
        send1[pl.ds(8 * i, 8), :] = jnp.where(upper, even[16:24], odd[16:24])
    hop1.start()

    w = w_ref[...]
    w_parts = thirds(w)
    r16, l16 = iota((256, 16), 0), iota((256, 16), 1)
    at_outer = one_hot(l16 == ((r16 >> 7) << 3) + ((r16 >> 3) & 7))
    at_inner = one_hot(l16 == (((r16 >> 6) & 1) << 3) + (r16 & 7))

    def spread(at):
        rows = nn(at, w_parts[0]) + nn(at, w_parts[1]) + nn(at, w_parts[2])
        return pick_exact(nt, thirds(rows), at)

    kw = split(spread(at_outer) * spread(at_inner))
    w_hi, w_lo = w_parts[0], w_parts[1]

    live1, own1, before1, parent1, octant1, group1 = links1
    att = iota((64, 128), 0)
    traits = (
        (own1 & (att == group1))
        | (before1 & (att == 16 + parent1))
        | (live1 & (att == 20 + (octant1 >> 2)))
        | (live1 & (att == 24 + (octant1 & 3)))
    )
    boxes = nt(slots2, one_hot(traits)).astype(BF16)
    rho, box = iota((160, 32), 0), iota((160, 32), 1)
    is_tail = rho >= 128
    rows_of = jnp.where(is_tail, 16 + (rho & 3), rho & 15)
    per_row = nn(one_hot(box == rows_of), boxes).astype(BF16)
    trait, col = iota((64, 768), 0), iota((64, 768), 1)
    prev_col, qr_col = col - 256, col - 384
    table = (
        ((col < 256) & (trait == (col & 15)))
        | ((col >= 256) & (col < 320) & (trait == 16 + (prev_col & 3)))
        | ((col >= 384) & (col < 640) & (trait == 24 + (qr_col >> 6)))
        | ((col >= 640) & (col < 656) & (trait == 20 + ((col - 640) >> 3)))
    )
    masks = nn(per_row, one_hot(table))
    rho16, y16 = iota((160, 128), 0), iota((160, 128), 1)
    own_index = jnp.where(rho16 >= 128, (rho16 - 128) >> 2, rho16 >> 4)
    choose = jnp.where((y16 & 7) == own_index, masks[:, 640:768], 0.0).astype(BF16)
    x384, c384 = iota((16, 384), 0), iota((16, 384), 1)
    p384 = c384 - 256
    fine = jnp.where(c384 < 256, c384 >> 4, (((p384 >> 2) & 1) << 3) + (p384 >> 3))
    columns = one_hot(x384 == fine)
    pad = jnp.zeros((112, 384), BF16)
    keep = masks[:, :384]

    def lifted(part):
        wide = jnp.concatenate([nn(part, columns).astype(BF16), pad], 0)
        return (nn(choose, wide) * keep).astype(BF16)

    up_hi, up_lo = lifted(w_hi), lifted(w_lo)
    own_up = (up_hi[:, :256], up_lo[:, :256])
    prev_up = (up_hi[:, 256:320], up_lo[:, 256:320])
    y1 = nt(x_hi[...], kw[0]) + nt(x_hi[...], kw[1])
    y1 = y1 + jnp.concatenate([nt(x_lo[...], kw[0]), jnp.zeros((128, 256), F32)], 0)
    v = triple(nn, own_up, split(y1))

    live2, own2, before2, parent2, octant2, group2 = links2
    row320, x320 = iota((320, 16), 0), iota((320, 16), 1)
    q320 = row320 - 256
    fine = jnp.where(row320 < 256, row320 >> 4, (((q320 >> 2) & 1) << 3) + (q320 >> 3))
    at_fine = one_hot(x320 == fine)
    down = (nt(at_fine, w_hi).astype(BF16), nt(at_fine, w_lo).astype(BF16))
    rows = iota((320, 128), 0)
    mine = ((rows < 256) & own2 & ((rows & 15) == group2)) | ((rows >= 256) & before2 & ((rows & 3) == parent2))
    y128 = iota((16, 128), 0)
    for i in range(8):
        which = one_hot(live2 & (y128 == ((octant2 >> 2) << 3) + i))
        as_hi[:, pl.ds(128 * i, 128)] = jnp.where(mine, nn(down[0], which), 0.0).astype(BF16)
        as_lo[:, pl.ds(128 * i, 128)] = jnp.where(mine, nn(down[1], which), 0.0).astype(BF16)

    det = nt(kw[0], x2[...]) + nt(kw[1], x2[...])
    quarter = [octant2 & 3 == q for q in range(4)]

    def gathered(block):
        parts = [jnp.where(quarter[q], block[64 * q : 64 * q + 64], 0.0) for q in range(4)]
        return (parts[0] + parts[1]) + (parts[2] + parts[3])

    hop0.wait_recv()
    tail_y = triple(nt, split(recv0[...]), kw)
    v = v + triple(nn, prev_up, split(tail_y))
    v = v * masks[:, 384:640]
    v = v[:, :128] + v[:, 128:]
    send2[...] = v[128:160]
    hop2.start()

    base = tuple(jnp.concatenate([k[:, :64], k[:, :64]], 1) for k in kw)
    own_scaled = triple(nt, base, split(v[:128]))
    y2 = split(jnp.concatenate([det[:, :128] + own_scaled, det[:, 128:]], 1))

    hop1.wait_recv()
    tail2 = recv1[...].astype(BF16)
    tail_det = split(nt(kw[0], tail2) + nt(kw[1], tail2))
    for i in range(8):
        lanes = pl.ds(128 * i, 128)
        block = triple(nn, y2, (as_hi[0:256, lanes], as_lo[0:256, lanes]))
        block = block + triple(nn, tail_det, (as_hi[256:320, lanes], as_lo[256:320, lanes]))
        out_ref[pl.ds(64 * i, 64), :] = gathered(block)

    hop2.wait_recv()
    r64, c64 = iota((64, 32), 0), iota((64, 32), 1)
    place = one_hot(r64 == ((c64 >> 2) << 3) + (c64 & 3))
    last = triple(nt, base, split(recv2[...]))
    l_hi, l_lo = split(last)
    last = (nt(l_hi, place).astype(BF16), nt(l_lo, place).astype(BF16))
    for i in range(8):
        lanes = pl.ds(128 * i, 128)
        block = triple(nn, last, (as_hi[256:320, lanes], as_lo[256:320, lanes]))
        out_ref[pl.ds(64 * i, 64), :] += gathered(block)

    hop0.wait_send()
    hop1.wait_send()
    hop2.wait_send()


def solution(mesh):
    leafs, subs = mesh.shape["leaf"], mesh.shape["sub"]

    def on_device(coarse_scaling, details, two_scale, parent_link):
        anywhere = pl.BlockSpec(memory_space=pl.ANY)
        inside = pl.BlockSpec(memory_space=pltpu.VMEM)
        tail = pltpu.VMEM((64, 256), F32)
        return pl.pallas_call(
            lambda *refs: kernel(leafs, subs, *refs),
            out_shape=jax.ShapeDtypeStruct(coarse_scaling.shape, F32),
            in_specs=[anywhere, anywhere, inside, inside],
            out_specs=inside,
            scratch_shapes=[
                pltpu.VMEM(coarse_scaling.shape, F32),
                pltpu.VMEM(details.shape, BF16),
                pltpu.VMEM((256, 256), BF16),
                pltpu.VMEM((128, 256), BF16),
                pltpu.VMEM((256, 256), BF16),
                pltpu.VMEM((320, 1024), BF16),
                pltpu.VMEM((320, 1024), BF16),
                tail, tail, tail, tail,
                pltpu.VMEM((32, 128), F32),
                pltpu.VMEM((32, 128), F32),
                pltpu.SemaphoreType.DMA((3,)),
                pltpu.SemaphoreType.DMA((3,)),
                pltpu.SemaphoreType.DMA((3,)),
            ],
            compiler_params=pltpu.CompilerParams(collective_id=0, has_side_effects=True),
            name="reconstruct",
        )(coarse_scaling, details, two_scale, parent_link)

    placed = (
        P(None, ("leaf", "sub")),
        P(None, None, ("leaf", "sub")),
        P(),
        P(None, ("leaf", "sub")),
    )
    return jax.shard_map(
        on_device, mesh=mesh, in_specs=placed, out_specs=P(None, ("leaf", "sub")), check_vma=False
    )
```

time: 164 us -> 32.4 us (0.20)
  the two profiles are of different devices: /device:TPU:14 before, /device:TPU:1 now
where the time goes in v1:
time: 32.4 us; the launch traced here: 32.2 us
  Pallas kernels  30.5 us (94%)
  local copies, waits for them, and re-layouts  1.67 us (5%)
    pallas_call x1, Pallas kernels, on_device(): pl.pallas_call(lambda *refs: kernel(leafs, subs, *refs), out_shape=jax.Sh...  30.5 us
    unnamed x1, local copies, waits for them, and re-layouts  1.67 us

profile of v1, /device:TPU:1, one launch (start us, length us, event | category | flops | bytes accessed | tf_op | source)
XLA Modules:
  0.0 32.2 jit_solution(14416974969144530781)
XLA Ops:
  0.0 30.5 %reconstruct.1 = f32[512,128]{1,0:T(8,128)} custom-call(f32[512,128]{1,0:T(8,128)} %refs_0_.1, bf16[2,3584,128]{2,1,0:T(8,128)(2,1)} %refs_1_.1, f32[16,16]{1,0:T(8,128)} %refs_2_.1, s32[2,128]{1,0:T(2,128)} %refs_3_.1), custom_call_target="tpu_custom_call" | custom-call | tf_op jit(solution)/shard_map/reconstruct/pallas_call | solution.py:269
  30.5 1.7 %copy.6 = f32[512,128]{1,0:T(8,128)} copy(f32[512,128]{1,0:T(8,128)} %reconstruct.1) | data formatting | bytes 524288

commit v2 on v0

v2 whole, which is shorter than its diff:
```python
import jax
import jax.numpy as jnp
from jax import lax
from jax.experimental import pallas as pl
from jax.experimental.pallas import tpu as pltpu
from jax.sharding import PartitionSpec as P

MESH = pl.DeviceIdType.MESH
TAIL = 4
F32, BF16, I32 = jnp.float32, jnp.bfloat16, jnp.int32


def iota(shape, axis):
    return lax.broadcasted_iota(I32, shape, axis)


def nn(a, b):
    return lax.dot_general(a, b, (((1,), (0,)), ((), ())), preferred_element_type=F32)


def nt(a, b):
    return lax.dot_general(a, b, (((1,), (1,)), ((), ())), preferred_element_type=F32)


def split(x):
    hi = x.astype(BF16)
    return hi, (x - hi.astype(F32)).astype(BF16)


def triple(dot, a, b):
    return dot(a[0], b[0]) + dot(a[1], b[0]) + dot(a[0], b[1])


def flag(mask):
    return jnp.where(mask, 1.0, 0.0)


def one_hot(mask):
    return flag(mask).astype(BF16)


def kernel(
    leafs, subs,
    coarse_hbm, details_hbm, w_hbm, link_hbm, out_ref,
    coarse, details, w_ref, link_ref, x_hi, x_lo, x2, as_hi, as_lo, mixed,
    up_hi, up_lo, quarter, p_hi, p_lo,
    send0, recv0, send1, recv1, send2, recv2, local_sem, send_sem, recv_sem,
):
    leaf, sub = lax.axis_index("leaf"), lax.axis_index("sub")
    device = leaf * subs + sub
    total = leafs * subs
    ahead = lax.rem(device + 1, total)
    behind = lax.rem(device + total - 1, total)
    target = (lax.div(ahead, subs), lax.rem(ahead, subs))
    source = (lax.div(behind, subs), lax.rem(behind, subs))
    has_source, has_target = device > 0, device < total - 1
    patient = sub < 2

    def load(n, src, dst):
        copy = pltpu.make_async_copy(src, dst, local_sem.at[n])
        copy.start()
        return copy

    load_link = load(0, link_hbm, link_ref)
    load_coarse = load(1, coarse_hbm, coarse)
    load_w = load(2, w_hbm, w_ref)
    load_first = []
    for c in range(4):
        rows = pl.ds(128 * c, 128)
        load_first.append(load(4 + c, details_hbm.at[0, :, rows, :], details.at[0, :, rows, :]))
    load_second = load(3, details_hbm.at[1], details.at[1])

    barrier = pltpu.get_barrier_semaphore()

    @pl.when(has_source)
    def _():
        pl.semaphore_signal(barrier, inc=1, device_id=source, device_id_type=MESH)

    def hop(n, src, dst):
        return pltpu.make_async_remote_copy(
            src_ref=src, dst_ref=dst, send_sem=send_sem.at[n], recv_sem=recv_sem.at[n],
            device_id=target, device_id_type=MESH,
        )

    hop0 = [hop(2 + c, send0.at[pl.ds(16 * c, 16), :], recv0.at[pl.ds(16 * c, 16), :]) for c in range(4)]
    hop1, hop2 = hop(0, send1, recv1), hop(1, send2, recv2)

    def fine(row):
        return (((row >> 3) & 1) << 3) + ((row >> 4) << 1) + ((row >> 2) & 1)

    first_child = device * 1024
    slot = iota((1, 128), 1)
    load_link.wait()

    def read_links(level):
        link = link_ref[level : level + 1, :]
        live = link >= 0
        own = link >= first_child
        offset = link - first_child
        parent = jnp.where(own, offset, offset + 8 * TAIL) >> 3
        octant = link & 7
        group = (slot - octant) >> 3
        return live, own, live & (link < first_child), parent, octant, group

    def parents_of(links):
        live, own, before, parent, octant, group = links
        start = own & (octant == 0)
        lead = one_hot(((slot >> 3) == iota((16, 128), 0)) & start)
        match = one_hot(iota((128, 128), 0) == parent)
        return nt(lead, match)

    links1, links2 = read_links(0), read_links(1)
    r16, s16 = iota((16, 128), 0), iota((16, 128), 1)
    tails = flag((r16 < 8) & (s16 == 128 - TAIL + (r16 & 3)))
    chosen1, chosen2 = parents_of(links1), parents_of(links2)
    pick1 = jnp.concatenate([chosen1, tails], 0).astype(BF16)
    pick2 = jnp.concatenate([chosen2, tails], 0).astype(BF16)

    upper = iota((8, 256), 0) < 4

    def stacked(level, a, i):
        first = 64 * i
        return [details[level, 4 * a + q - 1, pl.ds(first, 64), :] for q in range(4) if 4 * a + q]

    load_coarse.wait()
    no_rows = jnp.zeros((192, 128), BF16)
    pick1_twice = jnp.concatenate([pick1, pick1], 1)
    held = [None, None]
    for i in range(8):
        if i % 2 == 0:
            load_first[i // 2].wait()
        hi, lo = split(coarse[pl.ds(64 * i, 64), :])
        blocks = jnp.concatenate([hi] + stacked(0, 0, i), 0)
        lower = jnp.concatenate([lo, no_rows], 0)
        even = nt(pick1_twice, jnp.concatenate([blocks, lower], 1))
        odd = nt(pick1, jnp.concatenate(stacked(0, 1, i), 0))
        e_hi, e_lo = split(even[:16])
        x_hi[pl.ds(16 * i, 16), :] = e_hi
        x_lo[pl.ds(16 * i, 16), :] = e_lo
        x_hi[pl.ds(128 + 16 * i, 16), :] = odd[:16].astype(BF16)
        if i % 2:
            send0[pl.ds(8 * i - 8, 8), :] = jnp.where(upper, held[0], even[16:24])
            send0[pl.ds(8 * i, 8), :] = jnp.where(upper, held[1], odd[16:24])

            @pl.when(has_target & ~patient)
            def _(c=i // 2):
                if c == 0:
                    pl.semaphore_wait(barrier, 1)
                hop0[c].start()

        held = [even[16:24], odd[16:24]]

    load_second.wait()
    for i in range(8):
        even = nt(pick2, jnp.concatenate([jnp.zeros((64, 128), BF16)] + stacked(1, 0, i), 0))
        odd = nt(pick2, jnp.concatenate(stacked(1, 1, i), 0))
        x2[pl.ds(16 * i, 16), :] = even[:16].astype(BF16)
        x2[pl.ds(128 + 16 * i, 16), :] = odd[:16].astype(BF16)
        if i % 2:
            send1[pl.ds(8 * i - 8, 8), :] = jnp.where(upper, held[0], even[16:24])
            send1[pl.ds(8 * i, 8), :] = jnp.where(upper, held[1], odd[16:24])
        held = [even[16:24], odd[16:24]]

    @pl.when(has_target & ~patient)
    def _():
        hop1.start()

    load_w.wait()
    w = w_ref[...]
    w_hi, w_lo = split(w)
    row, lane = iota((256, 32), 0), iota((256, 32), 1)
    at_outer = one_hot((lane & 15) == ((row >> 7) << 3) + ((row >> 3) & 7))
    at_inner = one_hot((lane & 15) == (((row >> 6) & 1) << 3) + (row & 7))
    tall = jnp.concatenate([w_hi, w_lo], 0)
    wide = jnp.concatenate([tall, tall], 1)

    def spread(at):
        rows = nn(at, wide)
        top = rows.astype(BF16).astype(F32)
        return nt(jnp.where(lane < 16, top, rows - top).astype(BF16), at)

    kw = split(spread(at_outer) * spread(at_inner))

    live1, own1, before1, parent1, octant1, group1 = links1
    turned = jnp.concatenate([w[8:16], w[0:8]], 0)
    t_hi, t_lo = split(turned)
    x192, c192 = iota((16, 192), 0), iota((16, 192), 1)
    fits = x192 == fine(c192 & 63)
    middle = (c192 >> 6) == 1
    lift = nn(t_hi, one_hot(fits & ~middle)) + nn(t_lo, one_hot(fits & middle))
    lift = jnp.where((c192 & 3) == parent1[:, 127:128], lift, 0.0).astype(BF16)

    live2, own2, before2, parent2, octant2, group2 = links2
    base = tuple(jnp.concatenate([k[:, :64], k[:, :64]], 1) for k in kw)

    def folded(block, quarters):
        parts = [jnp.where(quarters == q, block[64 * q : 64 * q + 64], 0.0) for q in range(4)]
        return (parts[0] + parts[1]) + (parts[2] + parts[3])

    def own_work():
        att = iota((64, 128), 0)
        traits = (
            (own1 & (att == group1))
            | (before1 & (att == 16 + parent1))
            | (live1 & (att == 20 + (octant1 >> 2)))
            | (live1 & (att == 24 + (octant1 & 3)))
        )
        boxes = nt(chosen2.astype(BF16), one_hot(traits)).astype(BF16)
        per_row = nn(one_hot(iota((128, 16), 1) == (iota((128, 16), 0) & 15)), boxes).astype(BF16)
        trait, col = iota((64, 768), 0), iota((64, 768), 1)
        table = (
            ((col < 256) & (trait == (col & 15)))
            | ((col >= 256) & (col < 320) & (trait == 16 + (col & 3)))
            | ((col >= 384) & (col < 640) & (trait == 24 + ((col - 384) >> 6)))
            | ((col >= 640) & (col < 656) & (trait == 20 + ((col - 640) >> 3)))
        )
        masks = nn(per_row, one_hot(table))
        rho, y128 = iota((128, 128), 0), iota((128, 128), 1)
        choose = jnp.where((y128 & 7) == (rho >> 4), masks[:, 640:768], 0.0).astype(BF16)
        x384, c384 = iota((16, 384), 0), iota((16, 384), 1)
        columns = one_hot(x384 == jnp.where(c384 < 256, c384 >> 4, fine(c384 - 256)))
        pad = jnp.zeros((112, 384), BF16)
        keep = masks[:, :384]

        def lifted(part):
            rows = jnp.concatenate([nn(part, columns).astype(BF16), pad], 0)
            return (nn(choose, rows) * keep).astype(BF16)

        raised = lifted(w_hi), lifted(w_lo)
        up_hi[...], up_lo[...] = raised[0][:, 256:], raised[1][:, 256:]
        quarter[...] = masks[:, 384:640]
        own_up = (raised[0][:, :256], raised[1][:, :256])
        y1 = nt(x_hi[...], kw[0]) + nt(x_hi[...], kw[1])
        y1 = y1 + jnp.concatenate([nt(x_lo[...], kw[0]), jnp.zeros((128, 256), F32)], 0)
        v = triple(nn, own_up, split(y1)) * masks[:, 384:640]
        v = v[:, :128] + v[:, 128:]

        at_fine = one_hot(iota((256, 16), 1) == (iota((256, 16), 0) >> 4))
        down = (nt(at_fine, w_hi).astype(BF16), nt(at_fine, w_lo).astype(BF16))
        mine = own2 & ((iota((256, 128), 0) & 15) == group2)
        for i in range(8):
            which = one_hot(live2 & (r16 == ((octant2 >> 2) << 3) + i))
            as_hi[:, pl.ds(128 * i, 128)] = jnp.where(mine, nn(down[0], which), 0.0).astype(BF16)
            as_lo[:, pl.ds(128 * i, 128)] = jnp.where(mine, nn(down[1], which), 0.0).astype(BF16)

        det = nt(kw[0], x2[...]) + nt(kw[1], x2[...])
        own_scaled = triple(nt, base, split(v))
        y2 = split(jnp.concatenate([det[:, :128] + own_scaled, det[:, 128:]], 1))

        for i in range(8):
            lanes = pl.ds(128 * i, 128)
            block = triple(nn, y2, (as_hi[:, lanes], as_lo[:, lanes]))
            out_ref[pl.ds(64 * i, 64), :] = folded(block, octant2 & 3)

        names = one_hot(before2 & (parent2 == r16))
        c128 = iota((128, 256), 1)
        named = nn(names, one_hot(iota((128, 256), 0) == 96 + (c128 & 31))).astype(BF16)
        row96, x96 = iota((96, 16), 0), iota((96, 16), 1)
        late = row96 - 64
        comes = nn(one_hot(x96 == jnp.where(row96 < 64, row96 & 3, late >> 3)), named)
        at_prev = one_hot(x96 == jnp.where(row96 < 64, fine(row96 & 63), late & 7))
        c16 = iota((16, 256), 1)
        which = one_hot(iota((16, 256), 0) == (((c16 >> 2) & 1) << 3) + (c16 >> 5))

        def dropped(part):
            return (nn(nt(at_prev, part).astype(BF16), which) * comes).astype(BF16)

        p_hi[...], p_lo[...] = dropped(w_hi), dropped(w_lo)

    def messages():
        @pl.when(has_target & patient)
        def _():
            pl.semaphore_wait(barrier, 1)
            for copy in hop0:
                copy.start()
            hop1.start()

        @pl.when(has_source)
        def _():
            for copy in hop0:
                copy.wait_recv()
            hi, lo = split(recv0[...])
            mixed[...] = nn(lift, jnp.concatenate([hi, hi, lo], 0))[:8]

        @pl.when(device == 0)
        def _():
            recv0[...] = jnp.zeros((64, 256), F32)
            recv1[...] = jnp.zeros((64, 256), F32)
            recv2[...] = jnp.zeros((8, 256), F32)
            x256, c256 = iota((16, 256), 0), iota((16, 256), 1)
            fits = one_hot((x256 == (c256 >> 4)) & ((c256 & 15) == 15))
            l_hi, l_lo = nn(t_hi, fits).astype(BF16), nn(t_lo, fits).astype(BF16)
            both = nn(l_hi, x_hi[...]) + nn(l_lo, x_hi[...]) + nn(l_hi[:, :128], x_lo[...])
            mixed[...] = both[:8]

        @pl.when(has_target)
        def _():
            top = mixed[...].astype(BF16).astype(F32)
            pair = jnp.concatenate([top, mixed[...] - top], 0).astype(BF16)
            main = nt(pair, kw[0])
            send2[...] = main[:8] + main[8:] + nt(pair, kw[1])[:8]
            hop2.start()

    @pl.loop(0, 2)
    def _(n):
        turn = (n == 0) == patient
        pl.when(turn)(own_work)
        pl.when(jnp.logical_not(turn))(messages)

    tail_y = triple(nt, split(recv0[...]), kw)
    v = triple(nn, (up_hi[:, :64], up_lo[:, :64]), split(tail_y)) * quarter[...]
    v = v[:, :128] + v[:, 128:]
    s_hi, s_lo = split(triple(nt, base, split(v)))
    both = jnp.concatenate([s_hi, s_lo], 1)
    for i in range(8):
        lanes = pl.ds(128 * i, 128)
        top = as_hi[:128, lanes]
        block = nn(both, jnp.concatenate([top, top], 0)) + nn(s_hi, as_lo[:128, lanes])
        out_ref[pl.ds(64 * i, 64), :] += folded(block, octant2 & 3)

    scaled = jnp.concatenate([p_hi[64:, :], p_hi[64:, :], p_lo[64:, :]], 0)
    base4 = tuple(jnp.concatenate([b, b], 1) for b in base)
    static = iota((64, 256), 1) & 3
    reach = (iota((96, 256), 1) >> 6) == ((iota((96, 256), 0) >> 3) & 3)
    turn = iota((256, 96), 1) >> 5

    @pl.when(has_source)
    def _():
        hop1.wait_recv()
        tail2 = recv1[...].astype(BF16)
        tail_det = split(nt(kw[0], tail2) + nt(kw[1], tail2))
        prior = folded(triple(nn, tail_det, (p_hi[:64, :], p_lo[:64, :])), static)
        hop2.wait_recv()
        parts = split(jnp.where(reach, jnp.concatenate([recv2[...]] * 12, 0), 0.0))
        last = triple(nt, base4, parts)
        top = last.astype(BF16).astype(F32)
        block = nn(jnp.where(turn == 1, last - top, top).astype(BF16), scaled)
        block = prior + folded(block, static)
        for i in range(8):
            tile = block[:, 128 * (i // 4) : 128 * (i // 4) + 128]
            if i % 4 < 3:
                tile = pltpu.roll(tile, 96 - 32 * (i % 4), 1)
            rows = pl.ds(64 * i, 64)
            out_ref[rows, :] = jnp.where(before2, tile, out_ref[rows, :])

    @pl.when(has_target)
    def _():
        for copy in hop0 + [hop1, hop2]:
            copy.wait_send()


def solution(mesh):
    leafs, subs = mesh.shape["leaf"], mesh.shape["sub"]

    def on_device(coarse_scaling, details, two_scale, parent_link):
        outside = pl.BlockSpec(memory_space=pltpu.HBM)
        details = details.reshape(2, 7, 512, 128)
        tail = pltpu.VMEM((64, 256), F32)
        return pl.pallas_call(
            lambda *refs: kernel(leafs, subs, *refs),
            out_shape=jax.ShapeDtypeStruct(coarse_scaling.shape, F32),
            in_specs=[outside] * 4,
            out_specs=pl.BlockSpec(memory_space=pltpu.VMEM),
            scratch_shapes=[
                pltpu.VMEM(coarse_scaling.shape, F32),
                pltpu.VMEM(details.shape, BF16),
                pltpu.VMEM(two_scale.shape, F32),
                pltpu.VMEM(parent_link.shape, I32),
                pltpu.VMEM((256, 256), BF16),
                pltpu.VMEM((128, 256), BF16),
                pltpu.VMEM((256, 256), BF16),
                pltpu.VMEM((256, 1024), BF16),
                pltpu.VMEM((256, 1024), BF16),
                pltpu.VMEM((8, 256), F32),
                pltpu.VMEM((128, 128), BF16),
                pltpu.VMEM((128, 128), BF16),
                pltpu.VMEM((128, 256), F32),
                pltpu.VMEM((96, 256), BF16),
                pltpu.VMEM((96, 256), BF16),
                tail, tail, tail, tail,
                pltpu.VMEM((8, 256), F32),
                pltpu.VMEM((8, 256), F32),
                pltpu.SemaphoreType.DMA((8,)),
                pltpu.SemaphoreType.DMA((6,)),
                pltpu.SemaphoreType.DMA((6,)),
            ],
            compiler_params=pltpu.CompilerParams(
                collective_id=0, has_side_effects=True, vmem_limit_bytes=32 << 20
            ),
            name="reconstruct",
        )(*[pltpu.with_memory_space_constraint(a, pltpu.HBM) for a in (coarse_scaling, details, two_scale, parent_link)])

    placed = (
        P(None, ("leaf", "sub")),
        P(None, None, ("leaf", "sub")),
        P(),
        P(None, ("leaf", "sub")),
    )
    return jax.shard_map(
        on_device, mesh=mesh, in_specs=placed, out_specs=P(None, ("leaf", "sub")), check_vma=False
    )
```

time: 164 us -> 27.3 us (0.17)
  local copies, waits for them, and re-layouts: 105 us -> 0.71 us
  waiting for transfers between devices: 29.1 us -> 0 us
  Pallas kernels: 0 us -> 26.4 us
  matrix products: 17.6 us -> 0 us
  other arithmetic: 6.54 us -> 0 us
  starting transfers between devices: 3.84 us -> 0 us
    transpose x2 -> x0, local copies, waits for them, and re-layouts: 51.3 us -> none  [unfilter(): jnp.einsum('RMck,PIQJckn->IJMnPQR', halves, second_pass, precision=precise)]
    reshape x3 -> x0, local copies, waits for them, and re-layouts: 48 us -> none  [the longest x2 48 us: unfilter(): third_pass.reshape(poly_order * poly_order * poly_order, box_count * 8)]
    ppermute x2 -> x0, waiting for transfers between devices: 29.1 us -> none  [from_behind(): return lax.ppermute(x, axis, pairs)]
    pallas_call x0 -> x1, Pallas kernels: none -> 26.4 us  [on_device(): pl.pallas_call(lambda *refs: kernel(leafs, subs, *refs), out_shape=jax.Sh...]
    dot_general x6 -> x0, matrix products: 17.6 us -> none  [the longest x2 6.56 us: unfilter(): jnp.einsum('QJbj,PIbcjkn->PIQJckn', halves, first_pass, precision=precise)]
    gather x2 -> x0, local copies, waits for them, and re-layouts: 5.09 us -> none  [on_device(): picked = jnp.take(candidates, position, axis=1)]
    ppermute x2 -> x0, starting transfers between devices: 3.84 us -> none  [from_behind(): return lax.ppermute(x, axis, pairs)]
    concatenate x4 -> x0, other arithmetic: 3.34 us -> none  [the longest x2 3.07 us: on_device(): candidates = jnp.concatenate([own_children, received], 1)]
  transfers between devices with their start and end apart: 2 -> 0, of which waited for: 2 -> 0; matrix products, arithmetic and copies ran while one was open for 0% -> 0% of each run, Pallas kernels for 0% -> 0%
where the time goes in v2:
time: 27.3 us; the launch traced here: 27.1 us
  Pallas kernels  26.4 us (97%)
  local copies, waits for them, and re-layouts  0.71 us (3%)
    pallas_call x1, Pallas kernels, on_device(): pl.pallas_call(lambda *refs: kernel(leafs, subs, *refs), out_shape=jax.Sh...  26.4 us
    unnamed x1, local copies, waits for them, and re-layouts  0.71 us

profile of v2, /device:TPU:14, one launch (start us, length us, event | category | flops | bytes accessed | tf_op | source)
XLA Modules:
  0.0 27.1 jit_solution(9615303448800273477)
XLA Ops:
  0.0 26.4 %reconstruct.1 = f32[512,128]{1,0:T(8,128)S(1)} custom-call(f32[512,128]{1,0:T(8,128)} %refs_0_.1, bf16[2,7,512,128]{3,2,1,0:T(8,128)(2,1)} %bitcast.1, f32[16,16]{1,0:T(8,128)} %refs_2_.1, s32[2,128]{1,0:T(2,128)} %refs_3_.1), custom_call_target="tpu_custom_call" | custom-call | tf_op jit(solution)/shard_map/reconstruct/pallas_call | solution.py:359
  26.4 0.7 %copy.6 = f32[512,128]{1,0:T(8,128)} copy(f32[512,128]{1,0:T(8,128)S(1)} %reconstruct.1) | data formatting | bytes 524288

commit v3 on v2

--- a/solution.py
+++ b/solution.py
@@ -28,7 +28,14 @@
 
 
 def triple(dot, a, b):
-    return dot(a[0], b[0]) + dot(a[1], b[0]) + dot(a[0], b[1])
+    if a[0].shape[1] != 128:
+        return dot(a[0], b[0]) + dot(a[1], b[0]) + dot(a[0], b[1])
+    doubled = jnp.concatenate([b[0], b[0]], 0 if dot is nn else 1)
+    return dot(jnp.concatenate([a[0], a[1]], 1), doubled) + dot(a[0], b[1])
+
+
+def below(x, rows):
+    return jnp.concatenate([x, jnp.zeros((rows, x.shape[1]), x.dtype)], 0)
 
 
 def flag(mask):
@@ -123,34 +130,50 @@
         return [details[level, 4 * a + q - 1, pl.ds(first, 64), :] for q in range(4) if 4 * a + q]
 
     load_coarse.wait()
-    no_rows = jnp.zeros((192, 128), BF16)
-    pick1_twice = jnp.concatenate([pick1, pick1], 1)
+    first_half = iota((32, 128), 1) < 64
+
+    def parents_blocks(c):
+        hi, lo = split(coarse[pl.ds(128 * c, 128), :])
+        finer = nt(pick1, lo)
+        pairs = []
+        for n in range(2):
+            i = 2 * c + n
+            even = nt(pick1, jnp.concatenate([hi[64 * n : 64 * n + 64]] + stacked(0, 0, i), 0))
+            rest = jnp.where(first_half, pltpu.roll(finer, 64, 1) if n else finer, 0.0)
+            even = jnp.concatenate([even[:, :128] + rest, even[:, 128:]], 1)
+            pairs.append((even, nt(pick1, jnp.concatenate(stacked(0, 1, i), 0))))
+        return pairs
+
+    def keep_piece(c, pairs):
+        for i, (even, odd) in zip((2 * c, 2 * c + 1), pairs):
+            e_hi, e_lo = split(even[:16])
+            x_hi[pl.ds(16 * i, 16), :] = e_hi
+            x_lo[pl.ds(16 * i, 16), :] = e_lo
+            x_hi[pl.ds(128 + 16 * i, 16), :] = odd[:16].astype(BF16)
+
+    def send_piece(c, pairs):
+        for half in range(2):
+            first, second = pairs[0][half], pairs[1][half]
+            send0[pl.ds(16 * c + 8 * half, 8), :] = jnp.where(upper, first[16:24], second[16:24])
+
+        @pl.when(has_target & ~patient)
+        def _():
+            if c == 0:
+                pl.semaphore_wait(barrier, 1)
+            hop0[c].start()
+
+    pieces = []
+    for c in range(4):
+        load_first[c].wait()
+        pieces.append(parents_blocks(c))
+        if c:
+            send_piece(c - 1, pieces[c - 1])
+    send_piece(3, pieces[3])
+    for c in range(4):
+        keep_piece(c, pieces[c])
+
+    load_second.wait()
     held = [None, None]
-    for i in range(8):
-        if i % 2 == 0:
-            load_first[i // 2].wait()
-        hi, lo = split(coarse[pl.ds(64 * i, 64), :])
-        blocks = jnp.concatenate([hi] + stacked(0, 0, i), 0)
-        lower = jnp.concatenate([lo, no_rows], 0)
-        even = nt(pick1_twice, jnp.concatenate([blocks, lower], 1))
-        odd = nt(pick1, jnp.concatenate(stacked(0, 1, i), 0))
-        e_hi, e_lo = split(even[:16])
-        x_hi[pl.ds(16 * i, 16), :] = e_hi
-        x_lo[pl.ds(16 * i, 16), :] = e_lo
-        x_hi[pl.ds(128 + 16 * i, 16), :] = odd[:16].astype(BF16)
-        if i % 2:
-            send0[pl.ds(8 * i - 8, 8), :] = jnp.where(upper, held[0], even[16:24])
-            send0[pl.ds(8 * i, 8), :] = jnp.where(upper, held[1], odd[16:24])
-
-            @pl.when(has_target & ~patient)
-            def _(c=i // 2):
-                if c == 0:
-                    pl.semaphore_wait(barrier, 1)
-                hop0[c].start()
-
-        held = [even[16:24], odd[16:24]]
-
-    load_second.wait()
     for i in range(8):
         even = nt(pick2, jnp.concatenate([jnp.zeros((64, 128), BF16)] + stacked(1, 0, i), 0))
         odd = nt(pick2, jnp.concatenate(stacked(1, 1, i), 0))
@@ -231,7 +254,7 @@
         quarter[...] = masks[:, 384:640]
         own_up = (raised[0][:, :256], raised[1][:, :256])
         y1 = nt(x_hi[...], kw[0]) + nt(x_hi[...], kw[1])
-        y1 = y1 + jnp.concatenate([nt(x_lo[...], kw[0]), jnp.zeros((128, 256), F32)], 0)
+        y1 = y1 + below(nt(x_lo[...], kw[0]), 128)
         v = triple(nn, own_up, split(y1)) * masks[:, 384:640]
         v = v[:, :128] + v[:, 128:]
 
@@ -247,10 +270,11 @@
         own_scaled = triple(nt, base, split(v))
         y2 = split(jnp.concatenate([det[:, :128] + own_scaled, det[:, 128:]], 1))
 
-        for i in range(8):
-            lanes = pl.ds(128 * i, 128)
+        for i in range(0, 8, 2):
+            lanes = pl.ds(128 * i, 256)
             block = triple(nn, y2, (as_hi[:, lanes], as_lo[:, lanes]))
-            out_ref[pl.ds(64 * i, 64), :] = folded(block, octant2 & 3)
+            for n in range(2):
+                out_ref[pl.ds(64 * (i + n), 64), :] = folded(block[:, 128 * n : 128 * n + 128], octant2 & 3)
 
         names = one_hot(before2 & (parent2 == r16))
         c128 = iota((128, 256), 1)
@@ -308,31 +332,30 @@
         pl.when(jnp.logical_not(turn))(messages)
 
     tail_y = triple(nt, split(recv0[...]), kw)
-    v = triple(nn, (up_hi[:, :64], up_lo[:, :64]), split(tail_y)) * quarter[...]
+    v = triple(nn, (up_hi[...], up_lo[...]), split(below(tail_y, 64))) * quarter[...]
     v = v[:, :128] + v[:, 128:]
-    s_hi, s_lo = split(triple(nt, base, split(v)))
-    both = jnp.concatenate([s_hi, s_lo], 1)
-    for i in range(8):
-        lanes = pl.ds(128 * i, 128)
-        top = as_hi[:128, lanes]
-        block = nn(both, jnp.concatenate([top, top], 0)) + nn(s_hi, as_lo[:128, lanes])
-        out_ref[pl.ds(64 * i, 64), :] += folded(block, octant2 & 3)
+    scaling = split(triple(nt, base, split(v)))
+    for i in range(0, 8, 2):
+        lanes = pl.ds(128 * i, 256)
+        block = triple(nn, scaling, (as_hi[:128, lanes], as_lo[:128, lanes]))
+        for n in range(2):
+            out_ref[pl.ds(64 * (i + n), 64), :] += folded(block[:, 128 * n : 128 * n + 128], octant2 & 3)
 
     scaled = jnp.concatenate([p_hi[64:, :], p_hi[64:, :], p_lo[64:, :]], 0)
-    base4 = tuple(jnp.concatenate([b, b], 1) for b in base)
     static = iota((64, 256), 1) & 3
-    reach = (iota((96, 256), 1) >> 6) == ((iota((96, 256), 0) >> 3) & 3)
+    reach = (iota((96, 128), 1) >> 6) == ((iota((96, 128), 0) >> 3) & 1)
     turn = iota((256, 96), 1) >> 5
 
     @pl.when(has_source)
     def _():
         hop1.wait_recv()
-        tail2 = recv1[...].astype(BF16)
+        tail2 = below(recv1[...].astype(BF16), 64)
         tail_det = split(nt(kw[0], tail2) + nt(kw[1], tail2))
-        prior = folded(triple(nn, tail_det, (p_hi[:64, :], p_lo[:64, :])), static)
+        prior = folded(triple(nn, tail_det, (below(p_hi[:64, :], 64), below(p_lo[:64, :], 64))), static)
         hop2.wait_recv()
-        parts = split(jnp.where(reach, jnp.concatenate([recv2[...]] * 12, 0), 0.0))
-        last = triple(nt, base4, parts)
+        left, right = recv2[:, :128], recv2[:, 128:]
+        parts = split(jnp.where(reach, jnp.concatenate([left, left, right, right] * 3, 0), 0.0))
+        last = triple(nt, base, parts)
         top = last.astype(BF16).astype(F32)
         block = nn(jnp.where(turn == 1, last - top, top).astype(BF16), scaled)
         block = prior + folded(block, static)

time: 27.3 us -> 27 us (0.989)
  Pallas kernels: 26.4 us -> 26.1 us
where the time goes in v3:
time: 27 us; the launch traced here: 26.9 us
  Pallas kernels  26.1 us (97%)
  local copies, waits for them, and re-layouts  0.71 us (3%)
    pallas_call x1, Pallas kernels, on_device(): pl.pallas_call(lambda *refs: kernel(leafs, subs, *refs), out_shape=jax.Sh...  26.1 us
    unnamed x1, local copies, waits for them, and re-layouts  0.71 us

profile of v3, /device:TPU:14, one launch (start us, length us, event | category | flops | bytes accessed | tf_op | source)
XLA Modules:
  0.0 26.9 jit_solution(15104951909946254608)
XLA Ops:
  0.0 26.1 %reconstruct.1 = f32[512,128]{1,0:T(8,128)S(1)} custom-call(f32[512,128]{1,0:T(8,128)} %refs_0_.1, bf16[2,7,512,128]{3,2,1,0:T(8,128)(2,1)} %bitcast.1, f32[16,16]{1,0:T(8,128)} %refs_2_.1, s32[2,128]{1,0:T(2,128)} %refs_3_.1), custom_call_target="tpu_custom_call" | custom-call | tf_op jit(solution)/shard_map/reconstruct/pallas_call | solution.py:382
  26.2 0.7 %copy.6 = f32[512,128]{1,0:T(8,128)} copy(f32[512,128]{1,0:T(8,128)S(1)} %reconstruct.1) | data formatting | bytes 524288

commit v4 on v3

--- a/solution.py
+++ b/solution.py
@@ -341,24 +341,30 @@
         for n in range(2):
             out_ref[pl.ds(64 * (i + n), 64), :] += folded(block[:, 128 * n : 128 * n + 128], octant2 & 3)
 
-    scaled = jnp.concatenate([p_hi[64:, :], p_hi[64:, :], p_lo[64:, :]], 0)
+    top64, low64, top32, low32 = p_hi[:64, :], p_lo[:64, :], p_hi[64:, :], p_lo[64:, :]
+    main = jnp.concatenate([top64, top64, below(jnp.concatenate([top32, top32, low32], 0), 32)], 0)
+    extra = below(low64, 64)
     static = iota((64, 256), 1) & 3
-    reach = (iota((96, 128), 1) >> 6) == ((iota((96, 128), 0) >> 3) & 1)
-    turn = iota((256, 96), 1) >> 5
+    reach = (iota((128, 128), 1) >> 6) == ((iota((128, 128), 0) >> 3) & 1)
+    third = iota((256, 128), 1) >> 5
 
     @pl.when(has_source)
     def _():
         hop1.wait_recv()
-        tail2 = below(recv1[...].astype(BF16), 64)
-        tail_det = split(nt(kw[0], tail2) + nt(kw[1], tail2))
-        prior = folded(triple(nn, tail_det, (below(p_hi[:64, :], 64), below(p_lo[:64, :], 64))), static)
+        tail2 = recv1[...].astype(BF16)
+        tail2 = jnp.concatenate([tail2, tail2], 0)
+        det2 = nt(kw[0], tail2) + nt(kw[1], tail2)
+        det_top = det2.astype(BF16)
+        upper_part = det_top.astype(F32)
+        det_both = jnp.where(third < 2, upper_part, det2 - upper_part).astype(BF16)
         hop2.wait_recv()
         left, right = recv2[:, :128], recv2[:, 128:]
-        parts = split(jnp.where(reach, jnp.concatenate([left, left, right, right] * 3, 0), 0.0))
+        parts = split(jnp.where(reach, jnp.concatenate([left, left, right, right] * 4, 0), 0.0))
         last = triple(nt, base, parts)
         top = last.astype(BF16).astype(F32)
-        block = nn(jnp.where(turn == 1, last - top, top).astype(BF16), scaled)
-        block = prior + folded(block, static)
+        last = jnp.where(third == 1, last - top, top).astype(BF16)
+        block = nn(jnp.concatenate([det_both, last], 1), main) + nn(det_top, extra)
+        block = folded(block, static)
         for i in range(8):
             tile = block[:, 128 * (i // 4) : 128 * (i // 4) + 128]
             if i % 4 < 3:

time: 27 us -> 26.9 us (level)
  no operation moved by 1% of the time
where the time goes in v4:
time: 26.9 us; the launch traced here: 26.7 us
  Pallas kernels  26 us (97%)
  local copies, waits for them, and re-layouts  0.71 us (3%)
    pallas_call x1, Pallas kernels, on_device(): pl.pallas_call(lambda *refs: kernel(leafs, subs, *refs), out_shape=jax.Sh...  26 us
    unnamed x1, local copies, waits for them, and re-layouts  0.71 us

profile of v4, /device:TPU:14, one launch (start us, length us, event | category | flops | bytes accessed | tf_op | source)
XLA Modules:
  0.0 26.7 jit_solution(1157600217230635273)
XLA Ops:
  0.0 26.0 %reconstruct.1 = f32[512,128]{1,0:T(8,128)S(1)} custom-call(f32[512,128]{1,0:T(8,128)} %refs_0_.1, bf16[2,7,512,128]{3,2,1,0:T(8,128)(2,1)} %bitcast.1, f32[16,16]{1,0:T(8,128)} %refs_2_.1, s32[2,128]{1,0:T(2,128)} %refs_3_.1), custom_call_target="tpu_custom_call" | custom-call | tf_op jit(solution)/shard_map/reconstruct/pallas_call | solution.py:388
  26.0 0.7 %copy.6 = f32[512,128]{1,0:T(8,128)} copy(f32[512,128]{1,0:T(8,128)S(1)} %reconstruct.1) | data formatting | bytes 524288
